TPU v7x, 32 devices: a whole 2x2x4 slice. The times are simulated.
32 devices in a mesh: section: 2 (over y), wide: 8 (over z, core), narrow: 2 (over x).
Axes of the slice: x: 2, y: 2, z: 4, core: 2. Of those that a mesh axis runs over, the one named last changes fastest.
Arguments:
- hidden: bfloat16 [2, 1024, 24576], P('section', None, 'wide'), may hold values from -6 to 6
- down_weight: bfloat16 [12288, 24576], P('narrow', 'wide'), may hold values from -0.0390625 to 0.0390625
- residual: bfloat16 [2, 1024, 12288], P('section', None, 'narrow'), may hold values from -6 to 6
- ln_gain: float32 [12288], P('narrow'), may hold values from 0.5 to 1.5
- ln_bias: float32 [12288], P('narrow'), may hold values from -3 to 3
- qkv_weight: bfloat16 [12288, 24576], P('narrow', 'wide'), may hold values from -1 to 1
Outputs:
- stream: bfloat16 [2, 1024, 12288], P('section', 'wide', 'narrow')
- context: bfloat16 [2, 1024, 8192], P('section', 'narrow', 'wide')
All inputs are finite; a program needn't handle non-finite values.
Results may differ from a plain program's by a relative error of at most 0.007.
Values may be sent and summed in bfloat16 or wider, within the bound.
A program may use at most 320 MiB of HBM per device.

v0:
```python
import jax
import jax.numpy as jnp
from jax import lax
from jax.sharding import PartitionSpec as P

D = 12288
HDIM = 128


def from_behind(value, axis, steps):
    count = lax.axis_size(axis)
    pairs = [(source, (source + steps) % count) for source in range(count)]
    return lax.ppermute(value, axis, pairs)


def per_device(hidden, down_weight, residual, ln_gain, ln_bias, qkv_weight):
    inner = hidden[0]
    resid = residual[0]
    seq_len = inner.shape[0]
    wide_rows = seq_len // lax.axis_size("wide")
    wide_at = lax.axis_index("wide")
    contract = (((1,), (1,)), ((), ()))
    partial_ffn = lax.dot_general(inner, down_weight, contract, preferred_element_type=jnp.float32)
    summed = lax.psum(partial_ffn, "wide")
    mine = (resid.astype(jnp.float32) + summed).astype(jnp.bfloat16)
    arrived = from_behind(mine, "section", 1)
    own_rows = lax.dynamic_slice_in_dim(mine, wide_at * wide_rows, wide_rows, 0)
    values = arrived.astype(jnp.float32)
    totals, squares = lax.psum(
        (jnp.sum(values, axis=1), jnp.sum(values * values, axis=1)), "narrow"
    )
    mean = totals / D
    var = squares / D - mean * mean
    normed = (
        (values - mean[:, None]) * lax.rsqrt(var + 1e-05)[:, None] * ln_gain + ln_bias
    ).astype(jnp.bfloat16)
    heads_here = qkv_weight.shape[1] // (3 * HDIM)
    query_count = seq_len // lax.axis_size("narrow")
    narrow_at = lax.axis_index("narrow")
    joined = lax.psum(
        jnp.dot(normed, qkv_weight, preferred_element_type=jnp.float32), "narrow"
    ).astype(jnp.bfloat16)
    mine_joined = lax.dynamic_slice_in_dim(joined, narrow_at * query_count, query_count, 0)
    query = mine_joined.reshape(query_count, heads_here, 3, HDIM)[:, :, 0]
    pairs = joined.reshape(seq_len, heads_here, 3, HDIM)[:, :, 1:]
    keys = pairs[:, :, 0]
    vals = pairs[:, :, 1]
    scores = jnp.einsum("qhd,khd->hqk", query, keys, preferred_element_type=jnp.float32) / jnp.sqrt(
        jnp.float32(HDIM)
    )
    query_pos = narrow_at * query_count + lax.broadcasted_iota(jnp.int32, (query_count, seq_len), 0)
    key_pos = lax.broadcasted_iota(jnp.int32, (query_count, seq_len), 1)
    scores = jnp.where((key_pos <= query_pos)[None], scores, jnp.float32(-1e30))
    top = jnp.max(scores, axis=2, keepdims=True)
    expd = jnp.exp(scores - top)
    probs = (expd / jnp.sum(expd, axis=2, keepdims=True)).astype(jnp.bfloat16)
    attended = jnp.einsum("hqk,khd->qhd", probs, vals, preferred_element_type=jnp.float32).astype(
        jnp.bfloat16
    )
    attended = attended.reshape(query_count, heads_here * HDIM)
    return (own_rows[None], attended[None])


def solution(mesh):
    return jax.shard_map(
        per_device,
        mesh=mesh,
        in_specs=(
            P("section", None, "wide"),
            P("narrow", "wide"),
            P("section", None, "narrow"),
            P("narrow"),
            P("narrow"),
            P("narrow", "wide"),
        ),
        out_specs=(P("section", "wide", "narrow"), P("section", "narrow", "wide")),
        check_vma=False,
    )
```

profile of v0, /device:TPU:0, one launch (start us, length us, event | category | flops | bytes accessed | tf_op | source)
XLA Modules:
  0.0 1245.0 jit_solution(1324470787373891507)
XLA Ops:
  7.2 0.0 all-reduce.4.cloned.1.call-start
  7.2 46.9 %fusion.18 = f32[1024,6144]{1,0:T(8,128)} fusion(bf16[6144,3072]{1,0:T(8,128)(2,1)} %param.7, bf16[1,1024,3072]{2,1,0:T(8,128)(2,1)} %param.6), kind=kOutput, calls=%fused_computation.24 | convolution fusion | flops 38654705664 | bytes 69206016 | tf_op jit(solution)/shard_map/dot_general | solution.py:23
  54.1 0.0 all-reduce.4.cloned.1.call-update
  54.1 0.0 copy-start.1
  54.1 0.0 copy-start.2
  54.1 493.4 %all-reduce.4.cloned.1.call-done = f32[1024,6144]{1,0:T(8,128)} async-done(((f32[1024,6144]{1,0:T(8,128)}), f32[1024,6144]{1,0:T(8,128)}) %all-reduce.4.cloned.1.call-update) | async-done | bytes 25165840 | tf_op jit(solution)/shard_map/psum | solution.py:24
  547.5 17.2 %fusion.6 = bf16[1024,6144]{1,0:T(8,128)(2,1)} fusion(f32[1024,6144]{1,0:T(8,128)} %all-reduce.4.cloned.1.call-done, bf16[1,1024,6144]{2,1,0:T(8,128)(2,1)} %param.8), kind=kLoop, calls=%fused_computation.10 | loop fusion | flops 18874368 | bytes 50331648 | tf_op jit(solution)/shard_map/convert_element_type | solution.py:25
  564.7 1.5 collective-permute-start
  566.1 1.2 iota_compare_fusion
  567.3 2.7 dynamic-slice_bitcast_fusion
  570.0 266.8 %collective-permute-done = bf16[1024,6144]{1,0:T(8,128)(2,1)} collective-permute-done((bf16[1024,6144]{1,0:T(8,128)(2,1)}, bf16[1024,6144]{1,0:T(8,128)(2,1)}, u32[]{:S(2)}, u32[]{:S(2)}) %collective-permute-start) | collective-permute-done | bytes 12582944 | tf_op jit(solution)/shard_map/ppermute | solution.py:13
  836.8 8.5 convert_reduce_fusion
  845.3 5.0 all-reduce
  850.3 0.0 copy-done.1
  850.3 0.0 copy-done.2
  850.3 48.3 %fusion.8 = f32[1024,3072]{1,0:T(8,128)} fusion(bf16[6144,3072]{1,0:T(8,128)(2,1)} %param.11, bf16[1024,6144]{1,0:T(8,128)(2,1)} %collective-permute-done, f32[6144]{0:T(1024)S(1)} %copy-done.1, f32[6144]{0:T(1024)S(1)} %copy-done.2, f32[1024]{0:T(1024)S(1)} %get-tuple-element.11, f32[1024]{0:T(1024)S(1)} %get-tuple-element.10), kind=kOutput, calls=%fused_computation.15 | convolution fusion | flops 38692454400 | bytes 62971904 | tf_op jit(solution)/shard_map/dot_general | solution.py:41
  898.6 285.4 %all-reduce.5 = bf16[1024,3072]{1,0:T(8,128)(2,1)} all-reduce(f32[1024,3072]{1,0:T(8,128)} %fusion.8), channel_id=1, replica_groups=mesh['section'=2,'wide'=8,'narrow'=2] {'narrow'}, use_global_device_ids=true, to_apply=%region_5.0 | all-reduce | flops 3145728 | bytes 18874368 | tf_op jit(solution)/shard_map/psum | solution.py:40
  1184.0 8.6 copy.11
  1192.6 2.1 constant_dynamic-slice_fusion
  1194.7 2.8 copy.13
  1197.5 0.0 copy-start
  1197.5 10.1 fusion.20
  1207.6 0.0 copy-done
  1207.6 21.2 %fusion.24 = (f32[8,512]{1,0:T(8,128)S(1)}, f32[8,512,1024]{2,1,0:T(8,128)}) fusion(f32[8,512,1024]{2,1,0:T(8,128)} %fusion.20, pred[512,1024]{1,0:T(8,128)(4,1)S(1)} %copy-done), kind=kOutput, calls=%fused_computation.39 | output fusion | flops 25166848 | bytes 34095104 | tf_op jit(solution)/shard_map/sub | solution.py:55
  1228.8 8.0 fusion.21
  1236.9 1.3 copy.16
  (2 shorter events, 0.0 us)
Async XLA Ops:
  7.2 540.3 %all-reduce.4.cloned.1.call-start = ((), (), s32[]{:S(2)}) async-start(), calls=%async_computation | async-start | bytes 50331648 | tf_op jit(solution)/shard_map/psum | solution.py:24
  54.1 796.2 %copy-start.1 = (f32[6144]{0:T(1024)S(1)}, f32[6144]{0:T(1024)}, u32[]{:S(2)}) copy-start(f32[6144]{0:T(1024)} %param.10) | copy-start | bytes 73732
  54.1 796.2 %copy-start.2 = (f32[6144]{0:T(1024)S(1)}, f32[6144]{0:T(1024)}, u32[]{:S(2)}) copy-start(f32[6144]{0:T(1024)} %param.9) | copy-start | bytes 73732
  564.7 272.1 %collective-permute-start = (bf16[1024,6144]{1,0:T(8,128)(2,1)}, bf16[1024,6144]{1,0:T(8,128)(2,1)}, u32[]{:S(2)}, u32[]{:S(2)}) collective-permute-start(bf16[1024,6144]{1,0:T(8,128)(2,1)} %fusion.6), channel_id=1, source_target_pairs={{0,16},{16,0},{1,17},{17,1},{2,18},{18,2},{3,19},{19,3},{4,20},{20... | collective-permute-start | bytes 37748744 | tf_op jit(solution)/shard_map/ppermute | solution.py:13
  1197.5 10.1 copy-start
Sparse Core Ops, SparseCore 0:
  54.2 493.2 all-reduce.3
where the time goes:
time: 1250 us
  waiting for transfers between devices  760 us (61%)
  blocking collectives  290 us (23%)
  matrix products  113 us (9%)
  other arithmetic  48.1 us (4%)
  local copies, waits for them, and re-layouts  17.6 us (1%)
  between operations  14.1 us (1%)
    psum x1, waiting for transfers between devices, per_device(): summed = lax.psum(partial_ffn, 'wide')  493 us
    psum x1, blocking collectives, per_device(): lax.psum(jnp.dot(normed, qkv_weight, preferred_element_type=jnp.float32),...  285 us
    ppermute x1, waiting for transfers between devices, from_behind(): return lax.ppermute(value, axis, pairs)  267 us
    dot_general x1, matrix products, per_device(): jnp.dot(normed, qkv_weight, preferred_element_type=jnp.float32)  48.3 us
    dot_general x1, matrix products, per_device(): lax.dot_general(inner, down_weight, contract, preferred_element_type=jnp....  46.9 us
  transfers between devices with their start and end apart: 2, of which 2 were waited for; matrix products, arithmetic and copies ran while one was open for 0% of the time, Pallas kernels for 0%

commit v1 on v0

--- a/solution.py
+++ b/solution.py
@@ -21,7 +21,7 @@
     wide_at = lax.axis_index("wide")
     contract = (((1,), (1,)), ((), ()))
     partial_ffn = lax.dot_general(inner, down_weight, contract, preferred_element_type=jnp.float32)
-    summed = lax.psum(partial_ffn, "wide")
+    summed = jnp.sum(lax.all_gather(partial_ffn, "wide"), axis=0)
     mine = (resid.astype(jnp.float32) + summed).astype(jnp.bfloat16)
     arrived = from_behind(mine, "section", 1)
     own_rows = lax.dynamic_slice_in_dim(mine, wide_at * wide_rows, wide_rows, 0)

time: 1250 us -> 2490 us (1.99)
  waiting for transfers between devices: 760 us -> 1940 us
  other arithmetic: 48.1 us -> 118 us
    all_gather x0 -> x1, waiting for transfers between devices: none -> 1670 us  [per_device(): summed = jnp.sum(lax.all_gather(partial_ffn, 'wide'), axis=0)]
    psum x1 -> x0, waiting for transfers between devices: 493 us -> none  [per_device(): summed = lax.psum(partial_ffn, 'wide')]
    reduce_sum x0 -> x1, other arithmetic: none -> 70.2 us  [per_device(): summed = jnp.sum(lax.all_gather(partial_ffn, 'wide'), axis=0)]
where the time goes in v1:
time: 2490 us
  waiting for transfers between devices  1940 us (78%)
  blocking collectives  291 us (12%)
  other arithmetic  118 us (5%)
  matrix products  113 us (5%)
    all_gather x1, waiting for transfers between devices, per_device(): summed = jnp.sum(lax.all_gather(partial_ffn, 'wide'), axis=0)  1670 us
    psum x1, blocking collectives, per_device(): lax.psum(jnp.dot(normed, qkv_weight, preferred_element_type=jnp.float32),...  286 us
    ppermute x1, waiting for transfers between devices, from_behind(): return lax.ppermute(value, axis, pairs)  267 us
    reduce_sum x1, other arithmetic, per_device(): summed = jnp.sum(lax.all_gather(partial_ffn, 'wide'), axis=0)  70.2 us
  transfers between devices with their start and end apart: 2, of which 2 were waited for; matrix products, arithmetic and copies ran while one was open for 0% of the time, Pallas kernels for 0%

profile of v1, /device:TPU:0, one launch (start us, length us, event | category | flops | bytes accessed | tf_op | source)
XLA Modules:
  0.0 2491.5 jit_solution(4011111177427958687)
XLA Ops:
  7.2 0.0 all-gather.3.cloned.1.call-start
  7.2 46.8 %fusion.18 = f32[1024,6144]{1,0:T(8,128)} fusion(bf16[6144,3072]{1,0:T(8,128)(2,1)} %param.7, bf16[1,1024,3072]{2,1,0:T(8,128)(2,1)} %param.6), kind=kOutput, calls=%fused_computation.24 | convolution fusion | flops 38654705664 | bytes 69206016 | tf_op jit(solution)/shard_map/dot_general | solution.py:23
  54.0 0.0 all-gather.3.cloned.1.call-update
  54.0 1668.3 %all-gather.3.cloned.1.call-done = f32[8192,6144]{1,0:T(8,128)} async-done(((f32[1024,6144]{1,0:T(8,128)}), f32[8192,6144]{1,0:T(8,128)}) %all-gather.3.cloned.1.call-update) | async-done | bytes 201326608 | tf_op jit(solution)/shard_map/all_gather | solution.py:24
  1722.3 70.2 %reduce_sum.36 = f32[1024,6144]{1,0:T(8,128)} reduce(f32[8,1024,6144]{2,1,0:T(8,128)} %bitcast.2, f32[]{:T(128)} %constant.12.clone.1), dimensions={0}, to_apply=%region_0.0 | reduce | flops 44040192 | bytes 226492416 | tf_op jit(solution)/shard_map/reduce_sum | solution.py:24
  1792.5 0.0 copy-start.1
  1792.5 0.0 copy-start.2
  1792.5 17.1 fusion.6
  1809.6 1.5 collective-permute-start
  1811.1 1.2 iota_compare_fusion
  1812.3 2.7 dynamic-slice_bitcast_fusion
  1815.0 267.5 %collective-permute-done = bf16[1024,6144]{1,0:T(8,128)(2,1)} collective-permute-done((bf16[1024,6144]{1,0:T(8,128)(2,1)}, bf16[1024,6144]{1,0:T(8,128)(2,1)}, u32[]{:S(2)}, u32[]{:S(2)}) %collective-permute-start) | collective-permute-done | bytes 12582944 | tf_op jit(solution)/shard_map/ppermute | solution.py:13
  2082.5 8.5 convert_reduce_fusion
  2090.9 5.0 all-reduce
  2096.0 0.0 copy-done.1
  2096.0 0.0 copy-done.2
  2096.0 48.2 %fusion.8 = f32[1024,3072]{1,0:T(8,128)} fusion(bf16[6144,3072]{1,0:T(8,128)(2,1)} %param.11, bf16[1024,6144]{1,0:T(8,128)(2,1)} %collective-permute-done, f32[6144]{0:T(1024)S(1)} %copy-done.1, f32[6144]{0:T(1024)S(1)} %copy-done.2, f32[1024]{0:T(1024)S(1)} %get-tuple-element.11, f32[1024]{0:T(1024)S(1)} %get-tuple-element.10), kind=kOutput, calls=%fused_computation.15 | convolution fusion | flops 38692454400 | bytes 62971904 | tf_op jit(solution)/shard_map/dot_general | solution.py:41
  2144.1 286.4 %all-reduce.2 = bf16[1024,3072]{1,0:T(8,128)(2,1)} all-reduce(f32[1024,3072]{1,0:T(8,128)} %fusion.8), channel_id=1, replica_groups=mesh['section'=2,'wide'=8,'narrow'=2] {'narrow'}, use_global_device_ids=true, to_apply=%region_5.0 | all-reduce | flops 3145728 | bytes 18874368 | tf_op jit(solution)/shard_map/psum | solution.py:40
  2430.5 8.6 copy.11
  2439.1 2.1 constant_dynamic-slice_fusion
  2441.2 2.8 copy.13
  2444.1 0.0 copy-start
  2444.1 10.0 fusion.20
  2454.1 0.0 copy-done
  2454.1 21.2 fusion.24
  2475.3 8.0 fusion.21
  2483.4 1.3 copy.16
  (2 shorter events, 0.0 us)
Async XLA Ops:
  7.2 1715.2 %all-gather.3.cloned.1.call-start = ((), (), s32[]{:S(2)}) async-start(), calls=%async_computation | async-start | bytes 226492416 | tf_op jit(solution)/shard_map/all_gather | solution.py:24
  1792.5 303.4 %copy-start.1 = (f32[6144]{0:T(1024)S(1)}, f32[6144]{0:T(1024)}, u32[]{:S(2)}) copy-start(f32[6144]{0:T(1024)} %param.10) | copy-start | bytes 73732
  1792.5 303.4 %copy-start.2 = (f32[6144]{0:T(1024)S(1)}, f32[6144]{0:T(1024)}, u32[]{:S(2)}) copy-start(f32[6144]{0:T(1024)} %param.9) | copy-start | bytes 73732
  1809.6 272.8 %collective-permute-start = (bf16[1024,6144]{1,0:T(8,128)(2,1)}, bf16[1024,6144]{1,0:T(8,128)(2,1)}, u32[]{:S(2)}, u32[]{:S(2)}) collective-permute-start(bf16[1024,6144]{1,0:T(8,128)(2,1)} %fusion.6), channel_id=1, source_target_pairs={{0,16},{16,0},{1,17},{17,1},{2,18},{18,2},{3,19},{19,3},{4,20},{20... | collective-permute-start | bytes 37748744 | tf_op jit(solution)/shard_map/ppermute | solution.py:13
  2444.1 10.1 copy-start
Sparse Core Ops, SparseCore 0:
  54.1 1668.1 all-gather.2
